TPU v7x, 32 devices: a whole 2x2x4 slice. The times are simulated.
32 devices in a mesh: groups: 2 (over y), seq: 4 (over z), exp: 4 (over x, core).
Axes of the slice: x: 2, y: 2, z: 4, core: 2. Of those that a mesh axis runs over, the one named last changes fastest.
Arguments:
- residual: bfloat16 [1024, 6144], P(('groups', 'seq'), 'exp'), parts along dimension 0, may hold values from -6 to 6
- query_rows: bfloat16 [1024, 6144], P(('groups', 'seq'), 'exp'), parts along dimension 0, may hold values from -6 to 6
- key_rows: bfloat16 [1024, 6144], P(('groups', 'seq'), 'exp'), parts along dimension 0, may hold values from -6 to 6
- value_rows: bfloat16 [1024, 6144], P(('groups', 'seq'), 'exp'), parts along dimension 0, may hold values from -6 to 6
- log_decay: float32 [1024, 48], P(('groups', 'seq'), 'exp'), parts along dimension 0, may hold values from -0.8 to 0
- attn_gain: float32 [6144], P('exp'), may hold values from 0.1 to 1.9
- norm_gain: float32 [6144], P('exp'), may hold values from 0.1 to 1.9
- router: bfloat16 [6144, 32], P('exp'), may hold values from -0.3125 to 0.3125
- expert_ids: int32 [1024, 2], P(('groups', 'seq')), parts along dimension 0, may hold values from 0 to 31, all different within a row
- priority: int32 [8, 128], P(('groups', 'seq')), parts along dimension 0, may hold values from 0 to 127, each once within a row
- gate_weight: bfloat16 [4, 6144, 4608], P('exp', None, 'seq'), may hold values from -0.078125 to 0.078125
- up_weight: bfloat16 [4, 6144, 4608], P('exp', None, 'seq'), may hold values from -0.078125 to 0.078125
- down_weight: bfloat16 [4, 4608, 6144], P('exp', None, 'seq'), may hold values from -0.125 to 0.125
Outputs:
- layer_out: bfloat16 [1024, 6144], P(('groups', 'seq'), 'exp'), parts along dimension 0
There are 2 independent parts, one for each index of `groups`. A program takes and returns all parts, laid end to end along the dimension named above; an argument that names none is the same for every part. Nothing has to cross between parts.
Inputs may be any that keep to these rules, and one draw needn't show every extreme that they name: `expert_ids`: each row names two different experts; ids of 4 or more name experts whose weights are not given. `priority`: each row holds every number from 0 to 127 once.
All inputs are finite; a program needn't handle non-finite values.
Results may differ from a plain program's by a relative error of at most 0.0047.
Values may be sent and summed in bfloat16 or wider, within the bound.
No kernel may reach another device: no remote copies, remote signals or barrier semaphores. Data moves between devices by JAX's collectives and lax.ppermute only.
A program may use at most 128 MiB of HBM per device.

v0:
```python
import jax
import jax.numpy as jnp
from jax import lax
from jax.sharding import PartitionSpec as P

D = 6144
HEAD = 128
EXPERTS = 32
CAP = 8


def link_states(earlier, later):
    return (earlier[0] * later[0], later[0] * earlier[1] + later[1])


def body(
    residual,
    query_rows,
    key_rows,
    value_rows,
    log_decay,
    attn_gain,
    norm_gain,
    router,
    expert_ids,
    priority,
    gate_weight,
    up_weight,
    down_weight,
):
    rows = residual.shape[0]
    width = residual.shape[1]
    heads = width // HEAD
    held = lax.axis_size("exp")
    queries = query_rows.reshape(rows, heads, HEAD)
    keys_local = key_rows.reshape(rows, heads, HEAD)
    values = value_rows.reshape(rows, heads, HEAD)
    cumulative = jnp.cumsum(log_decay, axis=0)
    scores = jnp.einsum("thd,shd->hts", queries, keys_local, preferred_element_type=jnp.float32)
    causal = (jnp.arange(rows)[:, None] >= jnp.arange(rows)[None, :])[None]
    spread = cumulative.T[:, :, None] - cumulative.T[:, None, :]
    weights = jnp.where(causal, scores * jnp.exp(jnp.where(causal, spread, 0.0)), 0.0).astype(
        jnp.bfloat16
    )
    local_part = jnp.einsum("hts,shd->thd", weights, values, preferred_element_type=jnp.float32)
    to_end = jnp.exp(cumulative[-1][None, :] - cumulative)
    keyed = (keys_local.astype(jnp.float32) * to_end[:, :, None]).astype(jnp.bfloat16)
    block_state = jnp.einsum("thd,the->hde", keyed, values, preferred_element_type=jnp.float32)
    block_decay = jnp.exp(cumulative[-1])
    seq_count = lax.axis_size("seq")
    share_size = block_state.size // seq_count
    flat_state = block_state.reshape(seq_count, share_size)
    tiled_decay = jnp.broadcast_to(block_decay[None, :], (seq_count, heads))
    arrived_state, arrived_decay = (
        lax.all_to_all(flat_state, "seq", split_axis=0, concat_axis=0, tiled=True),
        lax.all_to_all(tiled_decay, "seq", split_axis=0, concat_axis=0, tiled=True),
    )
    position = lax.axis_index("seq") * share_size + jnp.arange(share_size, dtype=jnp.int32)
    owner_head = position // (HEAD * HEAD)
    selector = jnp.where(
        owner_head[None, :] == jnp.arange(heads, dtype=jnp.int32)[:, None], 1.0, 0.0
    ).astype(jnp.float32)
    element_decay = jnp.dot(arrived_decay, selector, precision=lax.Precision.HIGHEST)
    inclusive = lax.associative_scan(link_states, (element_decay, arrived_state), axis=0)[1]
    exclusive = jnp.concatenate([jnp.zeros((1, share_size), jnp.float32), inclusive[:-1]], axis=0)
    returned_prefix = lax.all_to_all(exclusive, "seq", split_axis=0, concat_axis=0, tiled=True)
    prior_state = returned_prefix.reshape(block_state.shape)
    inter = jnp.einsum(
        "thd,hde->the", queries.astype(jnp.float32), prior_state, precision=lax.Precision.HIGHEST
    )
    attended = local_part + jnp.exp(cumulative)[:, :, None] * inter
    normed = attended * lax.rsqrt(jnp.mean(attended * attended, axis=-1, keepdims=True) + 1e-06)
    normed = normed * attn_gain.reshape(heads, HEAD)
    mixed = (residual.astype(jnp.float32) + normed.reshape(rows, width)).astype(jnp.bfloat16)
    mixed_f = mixed.astype(jnp.float32)
    gained = mixed_f * norm_gain
    router_f = router.astype(jnp.float32)
    squares = lax.psum(jnp.sum(mixed_f * mixed_f, axis=1), "exp")
    inverse = lax.rsqrt(squares / D + 1e-06)
    scaled = gained * inverse[:, None]
    logits = lax.psum(jnp.dot(scaled, router_f, precision=lax.Precision.HIGHEST), "exp")
    tokens_in = scaled.astype(jnp.bfloat16)
    probs = jax.nn.sigmoid(logits)
    chosen = expert_ids[:, :, None] == jnp.arange(EXPERTS, dtype=jnp.int32)[None, None, :]
    selected = jnp.sum(jnp.where(chosen, probs[:, None, :], 0.0), axis=-1)
    gates = selected / jnp.sum(selected, axis=-1, keepdims=True)
    is_held = expert_ids[:, :, None] == jnp.arange(held, dtype=jnp.int32)[None, None, :]
    member = jnp.where(jnp.any(is_held, axis=1), 1.0, 0.0).astype(jnp.float32)
    gate_held = jnp.sum(jnp.where(is_held, gates[:, :, None], 0.0), axis=1)
    order = priority[0]
    earlier = jnp.where(order[None, :] < order[:, None], 1.0, 0.0).astype(jnp.bfloat16)
    rank = jnp.dot(earlier, member.astype(jnp.bfloat16), preferred_element_type=jnp.float32)
    kept = (member > 0.5) & (rank < CAP)
    slot_ids = jnp.arange(CAP).astype(jnp.float32)
    place = kept.T[:, None, :] & (rank.T[:, None, :] == slot_ids[None, :, None])
    place_f = jnp.where(place, 1.0, 0.0).astype(jnp.float32)
    buffer = jnp.einsum(
        "ect,td->ecd", place_f.astype(jnp.bfloat16), tokens_in, preferred_element_type=jnp.float32
    ).astype(jnp.bfloat16)
    arrived = lax.all_to_all(buffer, "exp", split_axis=0, concat_axis=2, tiled=True)[0]
    gathered = lax.all_gather(arrived, "seq", axis=0, tiled=True)
    gate = jnp.dot(gathered, gate_weight[0], preferred_element_type=jnp.float32)
    up = jnp.dot(gathered, up_weight[0], preferred_element_type=jnp.float32)
    hidden = (jax.nn.silu(gate) * up).astype(jnp.bfloat16)
    weight_rows = down_weight[0]
    summed = jnp.dot(
        lax.all_gather(hidden, "seq", axis=1, tiled=True),
        weight_rows,
        preferred_element_type=jnp.float32,
    )
    expert_out = summed.astype(jnp.bfloat16)
    returned = lax.all_to_all(expert_out, "seq", split_axis=0, concat_axis=1, tiled=True)
    regrouped = lax.all_to_all(returned[None], "exp", split_axis=2, concat_axis=0, tiled=True)
    weighted = place_f * gate_held.T[:, None, :]
    combined = jnp.einsum(
        "ect,ecd->td", weighted, regrouped.astype(jnp.float32), precision=lax.Precision.HIGHEST
    )
    return (mixed_f + combined).astype(jnp.bfloat16)


def solution(mesh):
    return jax.shard_map(
        body,
        mesh=mesh,
        in_specs=(
            P(("groups", "seq"), "exp"),
            P(("groups", "seq"), "exp"),
            P(("groups", "seq"), "exp"),
            P(("groups", "seq"), "exp"),
            P(("groups", "seq"), "exp"),
            P("exp"),
            P("exp"),
            P("exp", None),
            P(("groups", "seq"), None),
            P(("groups", "seq"), None),
            P("exp", None, "seq"),
            P("exp", None, "seq"),
            P("exp", None, "seq"),
        ),
        out_specs=P(("groups", "seq"), "exp"),
        check_vma=False,
    )
```

profile of v0, /device:TPU:0, one launch (start us, length us, event | category | flops | bytes accessed | tf_op | source)
XLA Modules:
  0.0 217.2 jit_solution(99139282639434964)
XLA Ops:
  1.6 6.3 %all-to-all-start.1 = ((f32[4,1,12]{2,1,0:T(1,128)}), f32[4,1,12]{2,1,0:T(1,128)S(1)}, u32[]{:S(2)}, u32[]{:S(2)}) async-start(f32[4,1,12]{2,1,0:T(1,128)} %broadcast_in_dim.109), calls=%async_computation.1 | async-start | bytes 4096 | tf_op jit(solution)/shard_map/all_to_all | solution.py:56
  11.8 1.7 all-to-all-done.1
  13.5 3.5 %all-to-all-start = ((f32[4,1,49152]{2,1,0:T(1,128)}), f32[4,1,49152]{2,1,0:T(1,128)S(1)}, u32[]{:S(2)}, u32[]{:S(2)}) async-start(f32[4,1,49152]{2,1,0:T(1,128)} %bitcast.6), calls=%async_computation | async-start | bytes 1572864 | tf_op jit(solution)/shard_map/all_to_all | solution.py:55
  17.1 1.9 fusion.6
  19.0 2.8 %slice.56 = f32[2,49152]{1,0:T(2,128)S(1)} slice(f32[4,49152]{1,0:T(4,128)S(1)} %fusion.6), slice={[1:4:2], [0:49152:1]} | slice | bytes 786432 | tf_op jit(solution)/shard_map/slice | solution.py:64
  21.9 5.1 %slice.60 = f32[2,49152]{1,0:T(2,128)} slice(f32[4,49152]{1,0:T(4,128)S(1)} %fusion.6), slice={[0:3:2], [0:49152:1]} | slice | bytes 786432 | tf_op jit(solution)/shard_map/slice | solution.py:64
  27.0 9.4 %all-to-all-done = f32[4,1,49152]{2,1,0:T(1,128)S(1)} async-done(((f32[4,1,49152]{2,1,0:T(1,128)}), f32[4,1,49152]{2,1,0:T(1,128)S(1)}, u32[]{:S(2)}, u32[]{:S(2)}) %all-to-all-start) | async-done | bytes 786464 | tf_op jit(solution)/shard_map/all_to_all | solution.py:55
  37.0 2.8 %slice.58 = f32[2,49152]{1,0:T(2,128)S(1)} slice(f32[4,49152]{1,0:T(4,128)S(1)} %bitcast.98), slice={[1:4:2], [0:49152:1]} | slice | bytes 786432 | tf_op jit(solution)/shard_map/slice | solution.py:64
  39.8 5.1 %slice.57 = f32[2,49152]{1,0:T(2,128)} slice(f32[4,49152]{1,0:T(4,128)S(1)} %bitcast.99), slice={[0:3:2], [0:49152:1]} | slice | bytes 786432 | tf_op jit(solution)/shard_map/slice | solution.py:64
  46.2 1.6 fusion.86
  48.1 1.7 fusion.52
  51.9 1.7 copy.119
  53.6 3.5 %all-to-all-start.2 = ((f32[4,1,49152]{2,1,0:T(1,128)}), f32[4,1,49152]{2,1,0:T(1,128)S(1)}, u32[]{:S(2)}, u32[]{:S(2)}) async-start(f32[4,1,49152]{2,1,0:T(1,128)} %copy.119), calls=%async_computation.2 | async-start | bytes 1572864 | tf_op jit(solution)/shard_map/all_to_all | solution.py:66
  58.7 18.0 %all-to-all-done.2 = f32[4,1,49152]{2,1,0:T(1,128)S(1)} async-done(((f32[4,1,49152]{2,1,0:T(1,128)}), f32[4,1,49152]{2,1,0:T(1,128)S(1)}, u32[]{:S(2)}, u32[]{:S(2)}) %all-to-all-start.2) | async-done | bytes 786464 | tf_op jit(solution)/shard_map/all_to_all | solution.py:66
  79.0 5.9 %psum.14 = f32[128]{0:T(128)S(1)} all-reduce(f32[128]{0:T(128)S(1)} %get-tuple-element.7), channel_id=1, replica_groups=mesh['groups'=2,'seq'=4,'exp'=4] {'exp'}, use_global_device_ids=true, to_apply=%region_4.5 | all-reduce | flops 128 | bytes 1024 | tf_op jit(solution)/shard_map/psum | solution.py:78
  85.7 3.5 %all-to-all-start.3 = ((bf16[4,8,1536]{2,1,0:T(8,128)(2,1)}), bf16[4,8,1536]{2,1,0:T(8,128)(2,1)S(1)}, u32[]{:S(2)}, u32[]{:S(2)}) async-start(bf16[4,8,1536]{2,1,0:T(8,128)(2,1)} %convolution_convert_fusion), calls=%async_computation.3 | async-start | bytes 196608 | tf_op jit(solution)/shard_map/all_to_all | solution.py:100
  89.9 11.7 %psum.15 = f32[128,32]{0,1:T(8,128)S(1)} all-reduce(f32[128,32]{0,1:T(8,128)S(1)} %fusion.31), channel_id=1, replica_groups=mesh['groups'=2,'seq'=4,'exp'=4] {'exp'}, use_global_device_ids=true, to_apply=%region_5.6 | all-reduce | flops 4096 | bytes 32768 | tf_op jit(solution)/shard_map/psum | solution.py:81
  101.7 14.8 %all_gather.6 = bf16[32,6144]{1,0:T(8,128)(2,1)S(1)} all-gather(bf16[8,6144]{1,0:T(8,128)(2,1)S(1)} %bitcast.110), channel_id=1, replica_groups=mesh['groups'=2,'seq'=4,'exp'=4] {'seq'}, dimensions={0}, use_global_device_ids=true | all-gather | bytes 491520 | tf_op jit(solution)/shard_map/all_gather | solution.py:101
  116.4 7.6 %fusion.4 = f32[32,1152]{1,0:T(8,128)S(1)} fusion(bf16[32,6144]{1,0:T(8,128)(2,1)S(1)} %all_gather.6, bf16[1,6144,1152]{2,1,0:T(8,128)(2,1)} %param.23), kind=kOutput, calls=%fused_computation.4 | convolution fusion | flops 452984832 | bytes 14696448 | tf_op jit(solution)/shard_map/dot_general | solution.py:102
  124.0 7.6 %fusion.13 = bf16[32,1152]{1,0:T(8,128)(2,1)S(1)} fusion(bf16[32,6144]{1,0:T(8,128)(2,1)S(1)} %all_gather.6, bf16[1,6144,1152]{2,1,0:T(8,128)(2,1)} %param.24, f32[32,1152]{1,0:T(8,128)S(1)} %fusion.4), kind=kOutput, calls=%fused_computation.13 | convolution fusion | flops 453206016 | bytes 14770176 | tf_op jit(solution)/shard_map/dot_general | solution.py:103
  131.6 13.9 %all_gather.7 = bf16[32,4608]{1,0:T(8,128)(2,1)S(1)} all-gather(bf16[32,1152]{1,0:T(8,128)(2,1)S(1)} %fusion.13), channel_id=1, replica_groups=mesh['groups'=2,'seq'=4,'exp'=4] {'seq'}, dimensions={1}, use_global_device_ids=true | all-gather | bytes 368640 | tf_op jit(solution)/shard_map/all_gather | solution.py:107
  145.5 3.2 %fusion.19 = bf16[4,8,1536]{2,1,0:T(8,128)(2,1)} fusion(bf16[32,4608]{1,0:T(8,128)(2,1)S(1)} %all_gather.7, bf16[1,4608,1536]{2,1,0:T(8,128)(2,1)S(1)} %bitcast.94), kind=kOutput, calls=%fused_computation.16 | convolution fusion | flops 453033984 | bytes 14548992 | tf_op jit(solution)/shard_map/dot_general | solution.py:106
  148.7 3.6 %all-to-all-start.4 = ((bf16[4,8,1536]{2,1,0:T(8,128)(2,1)}), bf16[4,8,1536]{2,1,0:T(8,128)(2,1)S(1)}, u32[]{:S(2)}, u32[]{:S(2)}) async-start(bf16[4,8,1536]{2,1,0:T(8,128)(2,1)} %fusion.19), calls=%async_computation.4 | async-start | bytes 196608 | tf_op jit(solution)/shard_map/all_to_all | solution.py:112
  152.3 5.8 %all-to-all-done.4 = bf16[4,8,1536]{2,1,0:T(8,128)(2,1)S(1)} async-done(((bf16[4,8,1536]{2,1,0:T(8,128)(2,1)}), bf16[4,8,1536]{2,1,0:T(8,128)(2,1)S(1)}, u32[]{:S(2)}, u32[]{:S(2)}) %all-to-all-start.4) | async-done | bytes 98336 | tf_op jit(solution)/shard_map/all_to_all | solution.py:112
  158.1 3.9 %copy.123 = bf16[1,8,6144]{1,0,2:T(2,128)(2,1)S(1)} copy(bf16[1,8,6144]{2,1,0:T(8,128)(2,1)S(1)} %bitcast.108) | data formatting | bytes 196608 | tf_op jit(solution)/shard_map/broadcast_in_dim | solution.py:113
  162.6 34.4 %reduce.1 = bf16[6144,8]{1,0:T(8,128)(2,1)} reduce(bf16[6144,1,8]{2,1,0:T(2,128)(2,1)S(1)} %bitcast.95, bf16[]{:T(256)} %broadcast.113), dimensions={1}, to_apply=%bitcast.78.reduce_sub_computation | reduce | bytes 196610
  197.1 3.7 %reshape.134 = bf16[4,2,6144]{2,1,0:T(2,128)(2,1)} reshape(bf16[6144,8]{1,0:T(8,128)(2,1)} %reduce.1) | data formatting | bytes 196608
  200.8 3.3 %all-to-all-start.5 = ((bf16[4,2,6144]{2,1,0:T(2,128)(2,1)}), bf16[4,2,6144]{2,1,0:T(2,128)(2,1)S(1)}, u32[]{:S(2)}, u32[]{:S(2)}) async-start(bf16[4,2,6144]{2,1,0:T(2,128)(2,1)} %reshape.134), calls=%async_computation.5 | async-start | bytes 196608 | tf_op jit(solution)/shard_map/all_to_all | solution.py:113
  204.1 4.2 %all-to-all-done.5 = bf16[4,2,6144]{2,1,0:T(2,128)(2,1)S(1)} async-done(((bf16[4,2,6144]{2,1,0:T(2,128)(2,1)}), bf16[4,2,6144]{2,1,0:T(2,128)(2,1)S(1)}, u32[]{:S(2)}, u32[]{:S(2)}) %all-to-all-start.5) | async-done | bytes 98336 | tf_op jit(solution)/shard_map/all_to_all | solution.py:113
  208.4 3.8 %reshape.135 = bf16[6144,1,8]{2,1,0:T(2,128)(2,1)S(1)} reshape(bf16[4,2,6144]{2,1,0:T(2,128)(2,1)S(1)} %all-to-all-done.5) | data formatting | bytes 196608
  212.2 2.7 %copy.124 = bf16[1,8,6144]{2,1,0:T(8,128)(2,1)S(1)} copy(bf16[1,8,6144]{1,0,2:T(2,128)(2,1)S(1)} %bitcast.96) | data formatting | bytes 196608 | tf_op jit(solution)/shard_map/all_to_all | solution.py:113
  214.9 2.4 %fusion.9 = bf16[128,1536]{1,0:T(8,128)(2,1)} fusion(bf16[4,8,1536]{2,1,0:T(8,128)(2,1)S(1)} %bitcast.109, bf16[128,1536]{1,0:T(8,128)(2,1)} %copy-done.2, f32[4,128]{1,0:T(4,128)S(1)} %bitcast.112, f32[4,128]{1,0:T(4,128)S(1)} %get-tuple-element.18, f32[8]{0:T(128)S(1)} %iota_convert_fusion, pred[4,128]{1,0:T(4,128)(4,1)S(1)} %get-tuple-element.17), kind=kOutput, calls=%fused_computation.11 | convolution fusion | flops 76103680 | bytes 889376 | tf_op jit(solution)/shard_map/ect,ecd->td/dot_general | solution.py:115
  (68 shorter events, 15.7 us)
Async XLA Ops:
  0.0 89.2 %copy-start = (bf16[1536,32]{0,1:T(8,128)(2,1)S(1)}, bf16[1536,32]{0,1:T(8,128)(2,1)}, u32[]{:S(2)}) copy-start(bf16[1536,32]{0,1:T(8,128)(2,1)} %param.20) | copy-start | bytes 294916
  1.0 57.4 %copy-start.6 = (s32[128,2]{0,1:T(2,128)S(1)}, s32[128,2]{0,1:T(2,128)}, u32[]{:S(2)}) copy-start(s32[128,2]{0,1:T(2,128)} %param.21) | copy-start | bytes 3076
  1.0 57.5 %copy-start.8 = (s32[1,128]{1,0:T(1,128)S(1)}, s32[1,128]{1,0:T(1,128)}, u32[]{:S(2)}) copy-start(s32[1,128]{1,0:T(1,128)} %param.22) | copy-start | bytes 1540
  1.6 11.8 %all-to-all-start.1 = ((f32[4,1,12]{2,1,0:T(1,128)}), f32[4,1,12]{2,1,0:T(1,128)S(1)}, u32[]{:S(2)}, u32[]{:S(2)}) async-start(f32[4,1,12]{2,1,0:T(1,128)} %broadcast_in_dim.109), calls=%async_computation.1 | async-start | bytes 4096 | tf_op jit(solution)/shard_map/all_to_all | solution.py:56
  13.5 23.0 %all-to-all-start = ((f32[4,1,49152]{2,1,0:T(1,128)}), f32[4,1,49152]{2,1,0:T(1,128)S(1)}, u32[]{:S(2)}, u32[]{:S(2)}) async-start(f32[4,1,49152]{2,1,0:T(1,128)} %bitcast.6), calls=%async_computation | async-start | bytes 1572864 | tf_op jit(solution)/shard_map/all_to_all | solution.py:55
  17.0 61.2 %copy-start.5 = (f32[1536]{0:T(1024)S(1)}, f32[1536]{0:T(1024)}, u32[]{:S(2)}) copy-start(f32[1536]{0:T(1024)} %param.18) | copy-start | bytes 18436
  19.0 8.0 %copy-start.3 = (f32[4,49152]{1,0:T(4,128)}, f32[4,49152]{1,0:T(4,128)S(1)}, u32[]{:S(2)}) copy-start(f32[4,49152]{1,0:T(4,128)S(1)} %fusion.6) | copy-start | bytes 2359300
  27.0 57.8 %copy-start.7 = (f32[1536]{0:T(1024)S(1)}, f32[1536]{0:T(1024)}, u32[]{:S(2)}) copy-start(f32[1536]{0:T(1024)} %param.19) | copy-start | bytes 18436
  46.2 32.6 %copy-start.4 = (bf16[128,1536]{1,0:T(8,128)(2,1)S(1)}, bf16[128,1536]{1,0:T(8,128)(2,1)}, u32[]{:S(2)}) copy-start(bf16[128,1536]{1,0:T(8,128)(2,1)} %param.13) | copy-start | bytes 1179652
  53.6 23.1 %all-to-all-start.2 = ((f32[4,1,49152]{2,1,0:T(1,128)}), f32[4,1,49152]{2,1,0:T(1,128)S(1)}, u32[]{:S(2)}, u32[]{:S(2)}) async-start(f32[4,1,49152]{2,1,0:T(1,128)} %copy.119), calls=%async_computation.2 | async-start | bytes 1572864 | tf_op jit(solution)/shard_map/all_to_all | solution.py:66
  79.0 52.6 %copy-start.2 = (bf16[128,1536]{1,0:T(8,128)(2,1)}, bf16[128,1536]{1,0:T(8,128)(2,1)S(1)}, u32[]{:S(2)}) copy-start(bf16[128,1536]{1,0:T(8,128)(2,1)S(1)} %get-tuple-element.8) | copy-start | bytes 1179652
  85.7 15.9 %all-to-all-start.3 = ((bf16[4,8,1536]{2,1,0:T(8,128)(2,1)}), bf16[4,8,1536]{2,1,0:T(8,128)(2,1)S(1)}, u32[]{:S(2)}, u32[]{:S(2)}) async-start(bf16[4,8,1536]{2,1,0:T(8,128)(2,1)} %convolution_convert_fusion), calls=%async_computation.3 | async-start | bytes 196608 | tf_op jit(solution)/shard_map/all_to_all | solution.py:100
  116.4 29.1 %slice-start = ((s8[14155776]{0:T(1024)(128)(4,1)}), s8[4194304]{0:T(1024)(128)(4,1)S(1)}, s32[]{:S(2)}) async-start(s8[14155776]{0:T(1024)(128)(4,1)} %bitcast.93), calls=%async_computation.6 | async-start | bytes 8388608
  116.4 29.1 %slice-start.1 = ((s8[14155776]{0:T(1024)(128)(4,1)}), s8[4194304]{0:T(1024)(128)(4,1)S(1)}, s32[]{:S(2)}) async-start(s8[14155776]{0:T(1024)(128)(4,1)} %bitcast.93), calls=%async_computation.7 | async-start | bytes 8388608
  124.0 21.5 %slice-start.2 = ((s8[14155776]{0:T(1024)(128)(4,1)}), s8[4194304]{0:T(1024)(128)(4,1)S(1)}, s32[]{:S(2)}) async-start(s8[14155776]{0:T(1024)(128)(4,1)} %bitcast.93), calls=%async_computation.8 | async-start | bytes 8388608
  124.0 21.5 %slice-start.3 = ((s8[14155776]{0:T(1024)(128)(4,1)}), s8[1572864]{0:T(1024)(128)(4,1)S(1)}, s32[]{:S(2)}) async-start(s8[14155776]{0:T(1024)(128)(4,1)} %bitcast.93), calls=%async_computation.9 | async-start | bytes 3145728
  145.5 71.7 %copy-start.1 = (bf16[1536,32]{0,1:T(8,128)(2,1)S(1)}, bf16[1536,32]{0,1:T(8,128)(2,1)}, u32[]{:S(2)}) copy-start(bf16[1536,32]{0,1:T(8,128)(2,1)} %param.20) | copy-start | bytes 294916
  148.7 9.4 %all-to-all-start.4 = ((bf16[4,8,1536]{2,1,0:T(8,128)(2,1)}), bf16[4,8,1536]{2,1,0:T(8,128)(2,1)S(1)}, u32[]{:S(2)}, u32[]{:S(2)}) async-start(bf16[4,8,1536]{2,1,0:T(8,128)(2,1)} %fusion.19), calls=%async_computation.4 | async-start | bytes 196608 | tf_op jit(solution)/shard_map/all_to_all | solution.py:112
  200.8 7.6 %all-to-all-start.5 = ((bf16[4,2,6144]{2,1,0:T(2,128)(2,1)}), bf16[4,2,6144]{2,1,0:T(2,128)(2,1)S(1)}, u32[]{:S(2)}, u32[]{:S(2)}) async-start(bf16[4,2,6144]{2,1,0:T(2,128)(2,1)} %reshape.134), calls=%async_computation.5 | async-start | bytes 196608 | tf_op jit(solution)/shard_map/all_to_all | solution.py:113
where the time goes:
time: 218 us; the launch traced here: 217 us
  blocking collectives  46.2 us (21%)
  other arithmetic  40.8 us (19%)
  local copies, waits for them, and re-layouts  39.9 us (18%)
  waiting for transfers between devices  39.2 us (18%)
  matrix products  27.1 us (12%)
  starting transfers between devices  23.7 us (11%)
    unnamed x2, other arithmetic  34.4 us
    all_to_all x1, waiting for transfers between devices, body(): lax.all_to_all(exclusive, 'seq', split_axis=0, concat_axis=0, tiled=True)  18 us
    slice x5, local copies, waits for them, and re-layouts, body(): lax.associative_scan(link_states, (element_decay, arrived_state), axis=0)[1]  15.9 us
    all_gather x1, blocking collectives, body(): gathered = lax.all_gather(arrived, 'seq', axis=0, tiled=True)  14.8 us
    all_gather x1, blocking collectives, body(): lax.all_gather(hidden, 'seq', axis=1, tiled=True)  13.9 us
    unnamed x35, local copies, waits for them, and re-layouts  13.7 us
    psum x1, blocking collectives, body(): lax.psum(jnp.dot(scaled, router_f, precision=lax.Precision.HIGHEST), 'exp')  11.7 us
    all_to_all x1, waiting for transfers between devices, body(): lax.all_to_all(flat_state, 'seq', split_axis=0, concat_axis=0, tiled=True)  9.43 us
  transfers between devices with their start and end apart: 6, of which 5 were waited for; matrix products, arithmetic and copies ran while one was open for 7% of the time, Pallas kernels for 0%

commit v1 on v0

--- a/solution.py
+++ b/solution.py
@@ -98,7 +98,12 @@
         "ect,td->ecd", place_f.astype(jnp.bfloat16), tokens_in, preferred_element_type=jnp.float32
     ).astype(jnp.bfloat16)
     arrived = lax.all_to_all(buffer, "exp", split_axis=0, concat_axis=2, tiled=True)[0]
-    gathered = lax.all_gather(arrived, "seq", axis=0, tiled=True)
+    ring = [arrived]
+    for hop in range(3):
+        ring.append(lax.ppermute(ring[-1], "seq", [(dev, (dev + 1) % 4) for dev in range(4)]))
+    gathered = jnp.roll(
+        jnp.concatenate(ring[::-1], axis=0), (lax.axis_index("seq") + 1) * ring[0].shape[0], axis=0
+    )
     gate = jnp.dot(gathered, gate_weight[0], preferred_element_type=jnp.float32)
     up = jnp.dot(gathered, up_weight[0], preferred_element_type=jnp.float32)
     hidden = (jax.nn.silu(gate) * up).astype(jnp.bfloat16)

time: 218 us -> 221 us (1.014)
  waiting for transfers between devices: 39.2 us -> 56.1 us
  blocking collectives: 46.2 us -> 30.3 us
    all_gather x1 -> x0, blocking collectives: 14.8 us -> none  [body(): gathered = lax.all_gather(arrived, 'seq', axis=0, tiled=True)]
    ppermute x0 -> x3, waiting for transfers between devices: none -> 12.8 us  [body(): lax.ppermute(ring[-1], 'seq', [(dev, (dev + 1) % 4) for dev in range(4)])]
    all_to_all x1, waiting for transfers between devices: 0.01 us -> 4.24 us  [body(): lax.all_to_all(buffer, 'exp', split_axis=0, concat_axis=2, tiled=True)[0]]
    unnamed x35 -> x42, local copies, waits for them, and re-layouts: 13.7 us -> 13.8 us
  transfers between devices with their start and end apart: 6 -> 9, of which waited for: 5 -> 8; matrix products, arithmetic and copies ran while one was open for 7% -> 7% of each run, Pallas kernels for 0% -> 0%
where the time goes in v1:
time: 221 us; the launch traced here: 220 us
  waiting for transfers between devices  56.1 us (25%)
  other arithmetic  40.8 us (18%)
  local copies, waits for them, and re-layouts  39.9 us (18%)
  blocking collectives  30.3 us (14%)
  matrix products  29.1 us (13%)
  starting transfers between devices  23.4 us (11%)
    unnamed x2, other arithmetic  34.5 us
    all_to_all x1, waiting for transfers between devices, body(): lax.all_to_all(exclusive, 'seq', split_axis=0, concat_axis=0, tiled=True)  18 us
    slice x5, local copies, waits for them, and re-layouts, body(): lax.associative_scan(link_states, (element_decay, arrived_state), axis=0)[1]  15.9 us
    all_gather x1, blocking collectives, body(): lax.all_gather(hidden, 'seq', axis=1, tiled=True)  14 us
    unnamed x42, local copies, waits for them, and re-layouts  13.8 us
    ppermute x3, waiting for transfers between devices, body(): lax.ppermute(ring[-1], 'seq', [(dev, (dev + 1) % 4) for dev in range(4)])  12.8 us
    psum x1, blocking collectives, body(): lax.psum(jnp.dot(scaled, router_f, precision=lax.Precision.HIGHEST), 'exp')  10.4 us
    all_to_all x1, waiting for transfers between devices, body(): lax.all_to_all(flat_state, 'seq', split_axis=0, concat_axis=0, tiled=True)  9.47 us
  transfers between devices with their start and end apart: 9, of which 8 were waited for; matrix products, arithmetic and copies ran while one was open for 7% of the time, Pallas kernels for 0%

profile of v1, /device:TPU:0, one launch (start us, length us, event | category | flops | bytes accessed | tf_op | source)
XLA Modules:
  0.0 220.2 jit_solution(14965681331085662758)
XLA Ops:
  1.6 6.3 %all-to-all-start.1 = ((f32[4,1,12]{2,1,0:T(1,128)}), f32[4,1,12]{2,1,0:T(1,128)S(1)}, u32[]{:S(2)}, u32[]{:S(2)}) async-start(f32[4,1,12]{2,1,0:T(1,128)} %broadcast_in_dim.109), calls=%async_computation.1 | async-start | bytes 4096 | tf_op jit(solution)/shard_map/all_to_all | solution.py:56
  13.5 3.5 %all-to-all-start = ((f32[4,1,49152]{2,1,0:T(1,128)}), f32[4,1,49152]{2,1,0:T(1,128)S(1)}, u32[]{:S(2)}, u32[]{:S(2)}) async-start(f32[4,1,49152]{2,1,0:T(1,128)} %bitcast.6), calls=%async_computation | async-start | bytes 1572864 | tf_op jit(solution)/shard_map/all_to_all | solution.py:55
  17.1 1.9 fusion.6
  19.0 2.8 %slice.56 = f32[2,49152]{1,0:T(2,128)S(1)} slice(f32[4,49152]{1,0:T(4,128)S(1)} %fusion.6), slice={[1:4:2], [0:49152:1]} | slice | bytes 786432 | tf_op jit(solution)/shard_map/slice | solution.py:64
  21.9 5.1 %slice.60 = f32[2,49152]{1,0:T(2,128)} slice(f32[4,49152]{1,0:T(4,128)S(1)} %fusion.6), slice={[0:3:2], [0:49152:1]} | slice | bytes 786432 | tf_op jit(solution)/shard_map/slice | solution.py:64
  27.0 9.5 %all-to-all-done = f32[4,1,49152]{2,1,0:T(1,128)S(1)} async-done(((f32[4,1,49152]{2,1,0:T(1,128)}), f32[4,1,49152]{2,1,0:T(1,128)S(1)}, u32[]{:S(2)}, u32[]{:S(2)}) %all-to-all-start) | async-done | bytes 786464 | tf_op jit(solution)/shard_map/all_to_all | solution.py:55
  37.0 2.8 %slice.58 = f32[2,49152]{1,0:T(2,128)S(1)} slice(f32[4,49152]{1,0:T(4,128)S(1)} %bitcast.94), slice={[1:4:2], [0:49152:1]} | slice | bytes 786432 | tf_op jit(solution)/shard_map/slice | solution.py:64
  39.8 5.1 %slice.57 = f32[2,49152]{1,0:T(2,128)} slice(f32[4,49152]{1,0:T(4,128)S(1)} %bitcast.95), slice={[0:3:2], [0:49152:1]} | slice | bytes 786432 | tf_op jit(solution)/shard_map/slice | solution.py:64
  51.9 1.7 copy.119
  53.6 3.5 %all-to-all-start.2 = ((f32[4,1,49152]{2,1,0:T(1,128)}), f32[4,1,49152]{2,1,0:T(1,128)S(1)}, u32[]{:S(2)}, u32[]{:S(2)}) async-start(f32[4,1,49152]{2,1,0:T(1,128)} %copy.119), calls=%async_computation.2 | async-start | bytes 1572864 | tf_op jit(solution)/shard_map/all_to_all | solution.py:66
  58.7 18.0 %all-to-all-done.2 = f32[4,1,49152]{2,1,0:T(1,128)S(1)} async-done(((f32[4,1,49152]{2,1,0:T(1,128)}), f32[4,1,49152]{2,1,0:T(1,128)S(1)}, u32[]{:S(2)}, u32[]{:S(2)}) %all-to-all-start.2) | async-done | bytes 786464 | tf_op jit(solution)/shard_map/all_to_all | solution.py:66
  78.4 1.8 multiply_reduce_fusion
  81.0 5.9 %psum.14 = f32[128]{0:T(128)S(1)} all-reduce(f32[128]{0:T(128)S(1)} %get-tuple-element.7), channel_id=1, replica_groups=mesh['groups'=2,'seq'=4,'exp'=4] {'exp'}, use_global_device_ids=true, to_apply=%region_4.5 | all-reduce | flops 128 | bytes 1024 | tf_op jit(solution)/shard_map/psum | solution.py:78
  87.8 3.5 %all-to-all-start.3 = ((bf16[4,8,1536]{2,1,0:T(8,128)(2,1)}), bf16[4,8,1536]{2,1,0:T(8,128)(2,1)S(1)}, u32[]{:S(2)}, u32[]{:S(2)}) async-start(bf16[4,8,1536]{2,1,0:T(8,128)(2,1)} %convolution_convert_fusion), calls=%async_computation.3 | async-start | bytes 196608 | tf_op jit(solution)/shard_map/all_to_all | solution.py:100
  91.3 4.2 %all-to-all-done.3 = bf16[4,8,1536]{2,1,0:T(8,128)(2,1)S(1)} async-done(((bf16[4,8,1536]{2,1,0:T(8,128)(2,1)}), bf16[4,8,1536]{2,1,0:T(8,128)(2,1)S(1)}, u32[]{:S(2)}, u32[]{:S(2)}) %all-to-all-start.3) | async-done | bytes 98336 | tf_op jit(solution)/shard_map/all_to_all | solution.py:100
  96.2 10.4 %psum.15 = f32[128,32]{0,1:T(8,128)S(1)} all-reduce(f32[128,32]{0,1:T(8,128)S(1)} %fusion.25), channel_id=1, replica_groups=mesh['groups'=2,'seq'=4,'exp'=4] {'exp'}, use_global_device_ids=true, to_apply=%region_5.6 | all-reduce | flops 4096 | bytes 32768 | tf_op jit(solution)/shard_map/psum | solution.py:81
  106.6 6.4 %collective-permute-done.1 = bf16[8,6144]{1,0:T(8,128)(2,1)S(1)} collective-permute-done((bf16[8,6144]{1,0:T(8,128)(2,1)S(1)}, bf16[8,6144]{1,0:T(8,128)(2,1)S(1)}, u32[]{:S(2)}, u32[]{:S(2)}) %collective-permute-start.1) | collective-permute-done | bytes 98336 | tf_op jit(solution)/shard_map/ppermute | solution.py:103
  113.1 6.4 %collective-permute-done.2 = bf16[8,6144]{1,0:T(8,128)(2,1)S(1)} collective-permute-done((bf16[8,6144]{1,0:T(8,128)(2,1)S(1)}, bf16[8,6144]{1,0:T(8,128)(2,1)S(1)}, u32[]{:S(2)}, u32[]{:S(2)}) %collective-permute-start.2) | collective-permute-done | bytes 98336 | tf_op jit(solution)/shard_map/ppermute | solution.py:103
  119.6 7.5 %fusion.4 = f32[32,1152]{1,0:T(8,128)S(1)} fusion(bf16[1,6144,1152]{2,1,0:T(8,128)(2,1)} %param.23, bf16[64,6144]{1,0:T(8,128)(2,1)S(1)} %constant_dynamic-update-slice_fusion, s32[]{:T(128)S(6)} %select_n.65), kind=kOutput, calls=%fused_computation.4 | convolution fusion | flops 452984832 | bytes 14696452 | tf_op jit(solution)/shard_map/dot_general | solution.py:107
  127.2 7.6 %multiply_convert_fusion.2 = bf16[32,1152]{1,0:T(8,128)(2,1)S(1)} fusion(f32[32,1152]{1,0:T(8,128)S(1)} %fusion.4, bf16[1,6144,1152]{2,1,0:T(8,128)(2,1)} %param.24, bf16[64,6144]{1,0:T(8,128)(2,1)S(1)} %constant_dynamic-update-slice_fusion, s32[]{:T(128)S(6)} %select_n.65), kind=kOutput, calls=%fused_computation.75 | convolution fusion | flops 453206016 | bytes 14770180 | tf_op jit(solution)/shard_map/dot_general | solution.py:108
  134.7 14.0 %all_gather.3 = bf16[32,4608]{1,0:T(8,128)(2,1)S(1)} all-gather(bf16[32,1152]{1,0:T(8,128)(2,1)S(1)} %multiply_convert_fusion.2), channel_id=1, replica_groups=mesh['groups'=2,'seq'=4,'exp'=4] {'seq'}, dimensions={1}, use_global_device_ids=true | all-gather | bytes 368640 | tf_op jit(solution)/shard_map/all_gather | solution.py:112
  148.8 3.2 %fusion.13 = bf16[4,8,1536]{2,1,0:T(8,128)(2,1)} fusion(bf16[32,4608]{1,0:T(8,128)(2,1)S(1)} %all_gather.3, bf16[1,4608,1536]{2,1,0:T(8,128)(2,1)S(1)} %bitcast.90), kind=kOutput, calls=%fused_computation.14 | convolution fusion | flops 453033984 | bytes 14548992 | tf_op jit(solution)/shard_map/dot_general | solution.py:111
  151.9 3.3 %all-to-all-start.4 = ((bf16[4,8,1536]{2,1,0:T(8,128)(2,1)}), bf16[4,8,1536]{2,1,0:T(8,128)(2,1)S(1)}, u32[]{:S(2)}, u32[]{:S(2)}) async-start(bf16[4,8,1536]{2,1,0:T(8,128)(2,1)} %fusion.13), calls=%async_computation.4 | async-start | bytes 196608 | tf_op jit(solution)/shard_map/all_to_all | solution.py:117
  155.3 5.8 %all-to-all-done.4 = bf16[4,8,1536]{2,1,0:T(8,128)(2,1)S(1)} async-done(((bf16[4,8,1536]{2,1,0:T(8,128)(2,1)}), bf16[4,8,1536]{2,1,0:T(8,128)(2,1)S(1)}, u32[]{:S(2)}, u32[]{:S(2)}) %all-to-all-start.4) | async-done | bytes 98336 | tf_op jit(solution)/shard_map/all_to_all | solution.py:117
  161.1 3.9 %copy.123 = bf16[1,8,6144]{1,0,2:T(2,128)(2,1)S(1)} copy(bf16[1,8,6144]{2,1,0:T(8,128)(2,1)S(1)} %bitcast.107) | data formatting | bytes 196608 | tf_op jit(solution)/shard_map/broadcast_in_dim | solution.py:118
  165.6 34.5 %reduce.1 = bf16[6144,8]{1,0:T(8,128)(2,1)} reduce(bf16[6144,1,8]{2,1,0:T(2,128)(2,1)S(1)} %bitcast.91, bf16[]{:T(256)} %broadcast.118), dimensions={1}, to_apply=%bitcast.76.reduce_sub_computation | reduce | bytes 196610
  200.0 3.7 %reshape.134 = bf16[4,2,6144]{2,1,0:T(2,128)(2,1)} reshape(bf16[6144,8]{1,0:T(8,128)(2,1)} %reduce.1) | data formatting | bytes 196608
  203.7 3.3 %all-to-all-start.5 = ((bf16[4,2,6144]{2,1,0:T(2,128)(2,1)}), bf16[4,2,6144]{2,1,0:T(2,128)(2,1)S(1)}, u32[]{:S(2)}, u32[]{:S(2)}) async-start(bf16[4,2,6144]{2,1,0:T(2,128)(2,1)} %reshape.134), calls=%async_computation.5 | async-start | bytes 196608 | tf_op jit(solution)/shard_map/all_to_all | solution.py:118
  207.1 4.2 %all-to-all-done.5 = bf16[4,2,6144]{2,1,0:T(2,128)(2,1)S(1)} async-done(((bf16[4,2,6144]{2,1,0:T(2,128)(2,1)}), bf16[4,2,6144]{2,1,0:T(2,128)(2,1)S(1)}, u32[]{:S(2)}, u32[]{:S(2)}) %all-to-all-start.5) | async-done | bytes 98336 | tf_op jit(solution)/shard_map/all_to_all | solution.py:118
  211.3 3.8 %reshape.135 = bf16[6144,1,8]{2,1,0:T(2,128)(2,1)S(1)} reshape(bf16[4,2,6144]{2,1,0:T(2,128)(2,1)S(1)} %all-to-all-done.5) | data formatting | bytes 196608
  215.1 2.7 %copy.124 = bf16[1,8,6144]{2,1,0:T(8,128)(2,1)S(1)} copy(bf16[1,8,6144]{1,0,2:T(2,128)(2,1)S(1)} %bitcast.92) | data formatting | bytes 196608 | tf_op jit(solution)/shard_map/all_to_all | solution.py:118
  217.8 2.4 %fusion.9 = bf16[128,1536]{1,0:T(8,128)(2,1)} fusion(bf16[4,8,1536]{2,1,0:T(8,128)(2,1)S(1)} %bitcast.108, bf16[128,1536]{1,0:T(8,128)(2,1)} %copy-done.2, f32[4,128]{1,0:T(4,128)S(1)} %bitcast.110, f32[4,128]{1,0:T(4,128)S(1)} %get-tuple-element.18, f32[8]{0:T(128)S(1)} %iota_convert_fusion, pred[4,128]{1,0:T(4,128)(4,1)S(1)} %get-tuple-element.17), kind=kOutput, calls=%fused_computation.11 | convolution fusion | flops 76103680 | bytes 889376 | tf_op jit(solution)/shard_map/ect,ecd->td/dot_general | solution.py:120
  (81 shorter events, 20.9 us)
Async XLA Ops:
  0.0 95.5 %copy-start = (bf16[1536,32]{0,1:T(8,128)(2,1)S(1)}, bf16[1536,32]{0,1:T(8,128)(2,1)}, u32[]{:S(2)}) copy-start(bf16[1536,32]{0,1:T(8,128)(2,1)} %param.20) | copy-start | bytes 294916
  1.0 57.4 %copy-start.6 = (s32[128,2]{0,1:T(2,128)S(1)}, s32[128,2]{0,1:T(2,128)}, u32[]{:S(2)}) copy-start(s32[128,2]{0,1:T(2,128)} %param.21) | copy-start | bytes 3076
  1.0 57.5 %copy-start.8 = (s32[1,128]{1,0:T(1,128)S(1)}, s32[1,128]{1,0:T(1,128)}, u32[]{:S(2)}) copy-start(s32[1,128]{1,0:T(1,128)} %param.22) | copy-start | bytes 1540
  1.6 11.8 %all-to-all-start.1 = ((f32[4,1,12]{2,1,0:T(1,128)}), f32[4,1,12]{2,1,0:T(1,128)S(1)}, u32[]{:S(2)}, u32[]{:S(2)}) async-start(f32[4,1,12]{2,1,0:T(1,128)} %broadcast_in_dim.109), calls=%async_computation.1 | async-start | bytes 4096 | tf_op jit(solution)/shard_map/all_to_all | solution.py:56
  13.5 23.0 %all-to-all-start = ((f32[4,1,49152]{2,1,0:T(1,128)}), f32[4,1,49152]{2,1,0:T(1,128)S(1)}, u32[]{:S(2)}, u32[]{:S(2)}) async-start(f32[4,1,49152]{2,1,0:T(1,128)} %bitcast.6), calls=%async_computation | async-start | bytes 1572864 | tf_op jit(solution)/shard_map/all_to_all | solution.py:55
  17.0 63.3 %copy-start.5 = (f32[1536]{0:T(1024)S(1)}, f32[1536]{0:T(1024)}, u32[]{:S(2)}) copy-start(f32[1536]{0:T(1024)} %param.18) | copy-start | bytes 18436
  19.0 8.0 %copy-start.3 = (f32[4,49152]{1,0:T(4,128)}, f32[4,49152]{1,0:T(4,128)S(1)}, u32[]{:S(2)}) copy-start(f32[4,49152]{1,0:T(4,128)S(1)} %fusion.6) | copy-start | bytes 2359300
  27.0 59.9 %copy-start.7 = (f32[1536]{0:T(1024)S(1)}, f32[1536]{0:T(1024)}, u32[]{:S(2)}) copy-start(f32[1536]{0:T(1024)} %param.19) | copy-start | bytes 18436
  46.2 34.6 %copy-start.4 = (bf16[128,1536]{1,0:T(8,128)(2,1)S(1)}, bf16[128,1536]{1,0:T(8,128)(2,1)}, u32[]{:S(2)}) copy-start(bf16[128,1536]{1,0:T(8,128)(2,1)} %param.13) | copy-start | bytes 1179652
  53.6 23.1 %all-to-all-start.2 = ((f32[4,1,49152]{2,1,0:T(1,128)}), f32[4,1,49152]{2,1,0:T(1,128)S(1)}, u32[]{:S(2)}, u32[]{:S(2)}) async-start(f32[4,1,49152]{2,1,0:T(1,128)} %copy.119), calls=%async_computation.2 | async-start | bytes 1572864 | tf_op jit(solution)/shard_map/all_to_all | solution.py:66
  81.0 53.8 %copy-start.2 = (bf16[128,1536]{1,0:T(8,128)(2,1)}, bf16[128,1536]{1,0:T(8,128)(2,1)S(1)}, u32[]{:S(2)}) copy-start(bf16[128,1536]{1,0:T(8,128)(2,1)S(1)} %get-tuple-element.8) | copy-start | bytes 1179652
  87.8 7.8 %all-to-all-start.3 = ((bf16[4,8,1536]{2,1,0:T(8,128)(2,1)}), bf16[4,8,1536]{2,1,0:T(8,128)(2,1)S(1)}, u32[]{:S(2)}, u32[]{:S(2)}) async-start(bf16[4,8,1536]{2,1,0:T(8,128)(2,1)} %convolution_convert_fusion), calls=%async_computation.3 | async-start | bytes 196608 | tf_op jit(solution)/shard_map/all_to_all | solution.py:100
  95.5 11.1 %collective-permute-start = (bf16[8,6144]{1,0:T(8,128)(2,1)S(1)}, bf16[8,6144]{1,0:T(8,128)(2,1)S(1)}, u32[]{:S(2)}, u32[]{:S(2)}) collective-permute-start(bf16[8,6144]{1,0:T(8,128)(2,1)S(1)} %bitcast.103), channel_id=1, source_target_pairs={{0,4},{4,8},{8,12},{12,0},{1,5},{5,9},{9,13},{13,1},{2,6},{6,10},{... | collective-permute-start | bytes 294920 | tf_op jit(solution)/shard_map/ppermute | solution.py:103
  106.6 6.4 %collective-permute-start.1 = (bf16[8,6144]{1,0:T(8,128)(2,1)S(1)}, bf16[8,6144]{1,0:T(8,128)(2,1)S(1)}, u32[]{:S(2)}, u32[]{:S(2)}) collective-permute-start(bf16[8,6144]{1,0:T(8,128)(2,1)S(1)} %collective-permute-done), channel_id=1, source_target_pairs={{0,4},{4,8},{8,12},{12,0},{1,5},{5,9},{9,13},{13,1},{2,6},{6,10},{... | collective-permute-start | bytes 294920 | tf_op jit(solution)/shard_map/ppermute | solution.py:103
  113.0 6.4 %collective-permute-start.2 = (bf16[8,6144]{1,0:T(8,128)(2,1)S(1)}, bf16[8,6144]{1,0:T(8,128)(2,1)S(1)}, u32[]{:S(2)}, u32[]{:S(2)}) collective-permute-start(bf16[8,6144]{1,0:T(8,128)(2,1)S(1)} %collective-permute-done.1), channel_id=1, source_target_pairs={{0,4},{4,8},{8,12},{12,0},{1,5},{5,9},{9,13},{13,1},{2,6},{6,10},{... | collective-permute-start | bytes 294920 | tf_op jit(solution)/shard_map/ppermute | solution.py:103
  119.6 29.2 %slice-start = ((s8[14155776]{0:T(1024)(128)(4,1)}), s8[4194304]{0:T(1024)(128)(4,1)S(1)}, s32[]{:S(2)}) async-start(s8[14155776]{0:T(1024)(128)(4,1)} %bitcast.89), calls=%async_computation.6 | async-start | bytes 8388608
  119.6 29.2 %slice-start.1 = ((s8[14155776]{0:T(1024)(128)(4,1)}), s8[4194304]{0:T(1024)(128)(4,1)S(1)}, s32[]{:S(2)}) async-start(s8[14155776]{0:T(1024)(128)(4,1)} %bitcast.89), calls=%async_computation.7 | async-start | bytes 8388608
  127.1 21.6 %slice-start.2 = ((s8[14155776]{0:T(1024)(128)(4,1)}), s8[4194304]{0:T(1024)(128)(4,1)S(1)}, s32[]{:S(2)}) async-start(s8[14155776]{0:T(1024)(128)(4,1)} %bitcast.89), calls=%async_computation.8 | async-start | bytes 8388608
  127.2 21.6 %slice-start.3 = ((s8[14155776]{0:T(1024)(128)(4,1)}), s8[1572864]{0:T(1024)(128)(4,1)S(1)}, s32[]{:S(2)}) async-start(s8[14155776]{0:T(1024)(128)(4,1)} %bitcast.89), calls=%async_computation.9 | async-start | bytes 3145728
  148.8 71.4 %copy-start.1 = (bf16[1536,32]{0,1:T(8,128)(2,1)S(1)}, bf16[1536,32]{0,1:T(8,128)(2,1)}, u32[]{:S(2)}) copy-start(bf16[1536,32]{0,1:T(8,128)(2,1)} %param.20) | copy-start | bytes 294916
  151.9 9.1 %all-to-all-start.4 = ((bf16[4,8,1536]{2,1,0:T(8,128)(2,1)}), bf16[4,8,1536]{2,1,0:T(8,128)(2,1)S(1)}, u32[]{:S(2)}, u32[]{:S(2)}) async-start(bf16[4,8,1536]{2,1,0:T(8,128)(2,1)} %fusion.13), calls=%async_computation.4 | async-start | bytes 196608 | tf_op jit(solution)/shard_map/all_to_all | solution.py:117
  203.7 7.6 %all-to-all-start.5 = ((bf16[4,2,6144]{2,1,0:T(2,128)(2,1)}), bf16[4,2,6144]{2,1,0:T(2,128)(2,1)S(1)}, u32[]{:S(2)}, u32[]{:S(2)}) async-start(bf16[4,2,6144]{2,1,0:T(2,128)(2,1)} %reshape.134), calls=%async_computation.5 | async-start | bytes 196608 | tf_op jit(solution)/shard_map/all_to_all | solution.py:118
